TPU v7x, 256 devices: a whole 4x4x8 slice. The times are simulated.
256 devices in a mesh: seg: 8 (over z_hi, core), shard: 16 (over x, y), tok: 2 (over z_lo).
Axes of the slice: x: 4, y: 4, z: 8 (z_hi: 4, z_lo: 2; z = z_hi * 2 + z_lo), core: 2. Of those that a mesh axis runs over, the one named last changes fastest.
Arguments:
- activations: bfloat16 [768, 2560], P('tok', 'shard'), may hold values from -6 to 6
- gate_weight: bfloat16 [2560, 10240], P('shard', 'seg'), may hold values from -0.125 to 0.125
- up_weight: bfloat16 [2560, 10240], P('shard', 'seg'), may hold values from -0.125 to 0.125
- down_weight: bfloat16 [10240, 2560], P('seg', 'shard'), may hold values from -0.0625 to 0.0625
- encoder_weight: bfloat16 [2560, 65536], P(None, ('seg', 'shard')), may hold values from -0.125 to 0.125
- encoder_bias: float32 [65536], P(('seg', 'shard')), may hold values from -0.6 to 0.2
- decoder_weight: bfloat16 [65536, 2560], P(('seg', 'shard')), may hold values from -0.0625 to 0.0625
- decoder_bias: float32 [2560], replicated, may hold values from -1.5 to 1.5
- segment_sizes: int32 [8], replicated, may hold values from 4096 to 8192, as said below
Outputs:
- grad_encoder: float32 [2560, 65536], P('tok', ('seg', 'shard'))
- grad_decoder: float32 [65536, 2560], P(('seg', 'shard'), 'tok')
- prefix_mse: float32 [8], P('seg')
Inputs may be any that keep to these rules, and one draw needn't show every extreme that they name: `segment_sizes`: at least one segment has all 8192 latents live.
All inputs are finite; a program needn't handle non-finite values.
Results may differ from a plain program's by a relative error of at most 0.0078.
Values may be sent and summed in bfloat16 or wider, within the bound.
No kernel may reach another device: no remote copies, remote signals or barrier semaphores. Data moves between devices by JAX's collectives and lax.ppermute only.
A program may use at most 64 MiB of HBM per device.

v0:
```python
import math
import jax
import jax.numpy as jnp
from jax import lax
from jax.sharding import PartitionSpec as P


def carried_in(value, axis, join, neutral, backward):
    count, mine = (lax.axis_size(axis), lax.axis_index(axis))
    pieces = lax.all_gather(value, axis)
    if backward:
        pieces = pieces[::-1]
        mine = count - 1 - mine
    subtotal = jnp.full_like(value, 0) + jnp.asarray(neutral, value.dtype)

    def hop(position, subtotal):
        longer = join(subtotal, pieces[position])
        return jnp.where(position < mine, longer, subtotal)

    return lax.fori_loop(0, count - 1, hop, subtotal)


def local(
    activations,
    gate_weight,
    up_weight,
    down_weight,
    encoder_weight,
    encoder_bias,
    decoder_weight,
    decoder_bias,
    segment_sizes,
):
    shard_index = lax.axis_index("shard")
    segment_index = lax.axis_index("seg")
    tok_rows = activations.shape[0]
    width_slice = activations.shape[1]
    gate_part = jnp.dot(activations, gate_weight, preferred_element_type=jnp.float32)
    up_part = jnp.dot(activations, up_weight, preferred_element_type=jnp.float32)
    gate_total, up_total = lax.psum((gate_part, up_part), "shard")
    hidden = (jax.nn.gelu(gate_total, approximate=True) * up_total).astype(jnp.bfloat16)
    down_part = jnp.dot(hidden, down_weight, preferred_element_type=jnp.float32)
    mlp_slice = lax.psum(down_part, "seg").astype(jnp.bfloat16)
    mlp_full = lax.all_gather(mlp_slice, "shard", axis=1, tiled=True)
    width = mlp_full.shape[1]
    groups = lax.axis_size("tok")
    tokens_all = tok_rows * groups
    mlp_float = mlp_full.astype(jnp.float32)
    centered = (mlp_float - decoder_bias).astype(jnp.bfloat16)
    lat_count = encoder_weight.shape[1]
    segment_total = segment_sizes.shape[0]
    size_here = jnp.sum(jnp.where(jnp.arange(segment_total) == segment_index, segment_sizes, 0))
    latent_index = shard_index * lat_count + jnp.arange(lat_count)
    live_mask = latent_index < size_here
    pre_act = jnp.dot(centered, encoder_weight, preferred_element_type=jnp.float32) + encoder_bias
    latent_codes = jnp.where(live_mask, jax.nn.softplus(10.0 * pre_act) / 10.0, 0.0).astype(
        jnp.bfloat16
    )
    slope = jnp.where(live_mask, jax.nn.sigmoid(10.0 * pre_act), 0.0)
    columns = decoder_weight
    my_part = lax.psum_scatter(
        lax.dot_general(
            columns, latent_codes, (((0,), (1,)), ((), ())), preferred_element_type=jnp.float32
        ),
        "shard",
        scatter_dimension=0,
        tiled=True,
    )
    column_start = shard_index * width_slice
    target = lax.dynamic_slice_in_dim(mlp_float, column_start, width_slice, 1).T
    bias_slice = lax.dynamic_slice_in_dim(decoder_bias, column_start, width_slice, 0)[:, None]
    blank = jnp.zeros_like(my_part)
    earlier = carried_in(my_part, "seg", jnp.add, blank, False)
    errors = bias_slice + (earlier + my_part) - target
    total_square = lax.psum(jnp.sum(errors * errors), ("shard", "tok"))
    prefix_mse = (total_square / (tokens_all * width)).reshape(1)
    later = carried_in(errors, "seg", jnp.add, blank, True)
    back = ((later + errors) * (1.0 / math.sqrt(tokens_all))).astype(jnp.bfloat16)
    piece = lax.all_gather(back, "shard", axis=0, tiled=True)
    columns = decoder_weight
    code_acc = lax.dot_general(
        piece, columns, (((0,), (1,)), ((), ())), preferred_element_type=jnp.float32
    )
    grad_piece = lax.dot_general(
        latent_codes, piece, (((0,), (1,)), ((), ())), preferred_element_type=jnp.float32
    )
    code_grad = (code_acc * slope).astype(jnp.bfloat16)
    encoder_grad = lax.dot_general(
        centered, code_grad, (((0,), (0,)), ((), ())), preferred_element_type=jnp.float32
    )
    grad_encoder = lax.psum_scatter(encoder_grad, "tok", scatter_dimension=0, tiled=True)
    grad_decoder = lax.psum_scatter(grad_piece, "tok", scatter_dimension=1, tiled=True)
    return (grad_encoder, grad_decoder, prefix_mse)


def solution(mesh):
    in_specs = (
        P("tok", "shard"),
        P("shard", "seg"),
        P("shard", "seg"),
        P("seg", "shard"),
        P(None, ("seg", "shard")),
        P(("seg", "shard")),
        P(("seg", "shard"), None),
        P(),
        P(),
    )
    out_specs = (P("tok", ("seg", "shard")), P(("seg", "shard"), "tok"), P("seg"))
    return jax.shard_map(local, mesh=mesh, in_specs=in_specs, out_specs=out_specs, check_vma=False)
```

profile of v0, /device:TPU:1, one launch (start us, length us, event | category | flops | bytes accessed | tf_op | source)
XLA Modules:
  0.0 602.7 jit_solution(8608097557932764812)
XLA Ops:
  7.2 2.9 fusion.35
  10.2 1.7 fusion.36
  12.0 0.0 all-gather.7.cloned.1.call-start
  12.0 114.8 %all-reduce.4.cloned.1.call-done = (f32[384,1280]{1,0:T(8,128)}, f32[384,1280]{1,0:T(8,128)}) async-done(((f32[384,1280]{1,0:T(8,128)}, f32[384,1280]{1,0:T(8,128)}), (f32[384,1280]{1,0:T(8,128)}, f32[384,1280]{1,0:T(8,128)})) %all-reduce.4.cloned.1.call-update) | async-done | bytes 3932176 | tf_op jit(solution)/shard_map/psum | solution.py:40
  126.8 3.1 fusion.12
  129.8 30.9 %all-reduce.5 = bf16[384,160]{0,1:T(8,128)(2,1)} all-reduce(f32[384,160]{0,1:T(8,128)S(1)} %fusion.12), channel_id=1, replica_groups=mesh['seg'=8,'shard'=16,'tok'=2] {'seg'}, use_global_device_ids=true, to_apply=%region_2.0 | all-reduce | flops 61440 | bytes 368640 | tf_op jit(solution)/shard_map/psum | solution.py:43
  160.7 0.0 reduce-scatter.4.cloned.1.call-start
  160.8 0.6 fusion.25
  161.4 0.7 add_compare_fusion
  162.1 47.5 %all-gather.7.cloned.1.call-done = bf16[384,2560]{0,1:T(8,128)(2,1)} async-done(((bf16[384,160]{0,1:T(8,128)(2,1)}), bf16[384,2560]{0,1:T(8,128)(2,1)}) %all-gather.7.cloned.1.call-update) | async-done | bytes 1966096 | tf_op jit(solution)/shard_map/all_gather | solution.py:44
  209.6 4.0 fusion.9
  213.6 0.9 copy-done.1
  214.5 3.6 convolution_bitcast_fusion
  218.2 0.0 all-gather.11.cloned.1.call-start
  218.2 82.0 %reduce-scatter.4.cloned.1.call-done = f32[160,384]{1,0:T(8,128)} async-done(((f32[2560,384]{1,0:T(8,128)}), f32[160,384]{1,0:T(8,128)}) %reduce-scatter.4.cloned.1.call-update) | async-done | bytes 245776 | tf_op jit(solution)/shard_map/reduce_scatter | solution.py:61
  300.2 0.0 all-gather.13.cloned.1.call-start
  300.3 0.1 dynamic_slice.20
  300.3 3.7 convert_element_type.23
  304.0 33.6 %all-gather.11.cloned.1.call-done = f32[1280,384]{1,0:T(8,128)} async-done(((f32[160,384]{1,0:T(8,128)}), f32[1280,384]{1,0:T(8,128)}) %all-gather.11.cloned.1.call-update) | async-done | bytes 1966096 | tf_op jit(solution)/shard_map/all_gather | solution.py:10
  337.6 7.2 %while.28 = (s32[]{:T(128)}, f32[160,384]{1,0:T(8,128)S(1)}, s32[]{:T(128)}, f32[8,160,384]{2,1,0:T(8,128)}, s32[]{:T(128)}, /*index=5*/s32[]{:T(128)}) while((s32[]{:T(128)}, f32[160,384]{1,0:T(8,128)S(1)}, s32[]{:T(128)}, f32[8,160,384]{2,1,0:T(8,128)}, s32[]{:T(128)}, /*index=5*/s32[]{:T(128)}) %tuple.87), condition=%wide.region_6.7_spmd.clone, body=%wide.region_5.6_spmd.clone.sunk | while | flops 184324 | bytes 737381 | solution.py:20
  337.6 1.0 add_select_fusion.4
  338.7 1.0 add_select_fusion.4
  339.7 1.0 add_select_fusion.4
  340.7 1.0 add_select_fusion.4
  341.8 1.0 add_select_fusion.4
  342.8 1.0 add_select_fusion.4
  343.9 1.0 add_select_fusion.4
  344.9 2.3 multiply_reduce_fusion
  347.2 0.0 all-gather.9.cloned.1.call-start
  347.3 33.5 %all-gather.13.cloned.1.call-done = f32[1280,384]{1,0:T(8,128)} async-done(((f32[160,384]{1,0:T(8,128)}), f32[1280,384]{1,0:T(8,128)}) %all-gather.13.cloned.1.call-update) | async-done | bytes 1966096 | tf_op jit(solution)/shard_map/all_gather | solution.py:10
  380.7 3.0 rev.3
  383.7 7.3 %while.29 = (s32[]{:T(128)}, f32[160,384]{1,0:T(8,128)S(1)}, s32[]{:T(128)}, f32[8,160,384]{2,1,0:T(8,128)}, s32[]{:T(128)}, /*index=5*/s32[]{:T(128)}) while((s32[]{:T(128)}, f32[160,384]{1,0:T(8,128)S(1)}, s32[]{:T(128)}, f32[8,160,384]{2,1,0:T(8,128)}, s32[]{:T(128)}, /*index=5*/s32[]{:T(128)}) %tuple.67), condition=%wide.region_8.9_spmd.clone, body=%wide.region_7.8_spmd.clone.sunk | while | flops 184324 | bytes 737381 | solution.py:20
  383.7 1.1 add_select_fusion.5
  384.8 1.0 add_select_fusion.5
  385.8 1.0 add_select_fusion.5
  386.8 1.0 add_select_fusion.5
  387.9 1.0 add_select_fusion.5
  388.9 1.0 add_select_fusion.5
  390.0 1.0 add_select_fusion.5
  391.0 0.7 multiply_convert_fusion
  391.7 0.0 reduce-scatter.6.cloned.1.call-start
  391.8 47.0 %all-gather.9.cloned.1.call-done = bf16[2560,384]{1,0:T(8,128)(2,1)} async-done(((bf16[160,384]{1,0:T(8,128)(2,1)}), bf16[2560,384]{1,0:T(8,128)(2,1)}) %all-gather.9.cloned.1.call-update) | async-done | bytes 1966096 | tf_op jit(solution)/shard_map/all_gather | solution.py:79
  438.7 7.3 %fusion.11 = f32[2560,512]{1,0:T(8,128)} fusion(bf16[2560,384]{1,0:T(8,128)(2,1)} %all-gather.9.cloned.1.call-done, bf16[512,2560]{1,0:T(8,128)(2,1)S(1)} %copy-done, f32[2560]{0:T(1024)S(1)} %copy-done.7, bf16[384,2560]{0,1:T(8,128)(2,1)} %all-gather.7.cloned.1.call-done, f32[384,512]{1,0:T(8,128)} %copy-done.1, pred[512]{0:T(512)(128)(4,1)S(1)} %add_compare_fusion), kind=kOutput, calls=%fused_computation.19 | convolution fusion | flops 2017394688 | bytes 12593664 | tf_op jit(solution)/shard_map/dot_general | solution.py:88
  446.1 0.0 reduce-scatter.8.cloned.1.call-start
  446.1 1.1 copy-done.2
  447.2 5.7 fusion.32
  453.0 71.1 %psum.31 = f32[]{:T(128)} all-reduce(f32[]{:T(128)} %get-tuple-element.211), channel_id=1, replica_groups=mesh['seg'=8,'shard'=16,'tok'=2] {'shard','tok'}, use_global_device_ids=true, to_apply=%region_12.13 | all-reduce | flops 1 | bytes 8 | tf_op jit(solution)/shard_map/psum | solution.py:75
  524.8 69.9 %reduce-scatter.8.cloned.1.call-done = f32[512,1280]{1,0:T(8,128)} async-done(((f32[512,2560]{1,0:T(8,128)}), f32[512,1280]{1,0:T(8,128)}) %reduce-scatter.8.cloned.1.call-update) | async-done | bytes 2621456 | tf_op jit(solution)/shard_map/reduce_scatter | solution.py:92
  (32 shorter events, 0.2 us)
Async XLA Ops:
  7.2 207.4 %copy-start = (bf16[512,2560]{1,0:T(8,128)(2,1)S(1)}, bf16[512,2560]{1,0:T(8,128)(2,1)}, u32[]{:S(2)}) copy-start(bf16[512,2560]{1,0:T(8,128)(2,1)} %param.19) | copy-start | bytes 7864324
  7.2 3.0 copy-start.5
  7.2 3.0 copy-start.6
  7.2 119.6 %all-reduce.4.cloned.1.call-start = ((), (), s32[]{:S(2)}) async-start(), calls=%async_computation.10 | async-start | bytes 7864320 | tf_op jit(solution)/shard_map/psum | solution.py:40
  11.9 114.8 %copy-start.8 = (bf16[1280,160]{0,1:T(8,128)(2,1)S(1)}, bf16[1280,160]{0,1:T(8,128)(2,1)}, u32[]{:S(2)}) copy-start(bf16[1280,160]{0,1:T(8,128)(2,1)} %param.16) | copy-start | bytes 1228804
  12.0 197.6 %all-gather.7.cloned.1.call-start = ((), (), s32[]{:S(2)}) async-start(), calls=%async_computation.3 | async-start | bytes 2088960 | tf_op jit(solution)/shard_map/all_gather | solution.py:44
  126.8 34.0 %copy-start.10 = (s32[8]{0:T(128)S(1)}, s32[8]{0:T(128)}, u32[]{:S(2)}) copy-start(s32[8]{0:T(128)} %param.21) | copy-start | bytes 100
  126.8 82.8 %copy-start.7 = (f32[2560]{0:T(1024)S(1)}, f32[2560]{0:T(1024)}, u32[]{:S(2)}) copy-start(f32[2560]{0:T(1024)} %param.20) | copy-start | bytes 30724
  126.8 82.8 %copy-start.9 = (f32[512]{0:T(512)S(1)}, f32[512]{0:T(512)}, u32[]{:S(2)}) copy-start(f32[512]{0:T(512)} %param.18) | copy-start | bytes 6148
  160.7 139.5 %reduce-scatter.4.cloned.1.call-start = ((), (), s32[]{:S(2)}) async-start(), calls=%async_computation.4 | async-start | bytes 4177920 | tf_op jit(solution)/shard_map/reduce_scatter | solution.py:61
  213.6 0.9 copy-start.1
  218.2 119.5 %all-gather.11.cloned.1.call-start = ((), (), s32[]{:S(2)}) async-start(), calls=%async_computation.8 | async-start | bytes 2211840 | tf_op jit(solution)/shard_map/all_gather | solution.py:10
  300.2 80.5 %all-gather.13.cloned.1.call-start = ((), (), s32[]{:S(2)}) async-start(), calls=%async_computation.9 | async-start | bytes 2211840 | tf_op jit(solution)/shard_map/all_gather | solution.py:10
  304.0 40.9 %copy-start.4 = (f32[160,384]{1,0:T(8,128)S(1)}, f32[160,384]{1,0:T(8,128)}, u32[]{:S(2)}) copy-start(f32[160,384]{1,0:T(8,128)} %reduce-scatter.4.cloned.1.call-done) | copy-start | bytes 737284
  347.2 91.5 %all-gather.9.cloned.1.call-start = ((), (), s32[]{:S(2)}) async-start(), calls=%async_computation.5 | async-start | bytes 2088960 | tf_op jit(solution)/shard_map/all_gather | solution.py:79
  383.7 7.3 %copy-start.3 = (f32[160,384]{1,0:T(8,128)S(1)}, f32[160,384]{1,0:T(8,128)}, u32[]{:S(2)}) copy-start(f32[160,384]{1,0:T(8,128)} %get-tuple-element.212) | copy-start | bytes 737284
  391.7 133.0 %reduce-scatter.6.cloned.1.call-start = ((), (), s32[]{:S(2)}) async-start(), calls=%async_computation.6 | async-start | bytes 7864320 | tf_op jit(solution)/shard_map/reduce_scatter | solution.py:91
  446.1 1.1 copy-start.2
  446.1 148.6 %reduce-scatter.8.cloned.1.call-start = ((), (), s32[]{:S(2)}) async-start(), calls=%async_computation.7 | async-start | bytes 7864320 | tf_op jit(solution)/shard_map/reduce_scatter | solution.py:92
Sparse Core Ops, SparseCore 0:
  12.1 114.6 all-reduce.3
  160.8 48.6 all-gather.6
  218.3 81.8 reduce-scatter.3
  301.9 35.7 all-gather.10
  347.3 33.3 all-gather.12
  391.8 46.8 all-gather.8
  446.2 73.8 reduce-scatter.5
  523.2 71.4 reduce-scatter.7
where the time goes:
time: 603 us
  waiting for transfers between devices  428 us (71%)
  blocking collectives  102 us (17%)
  matrix products  28.5 us (5%)
  other arithmetic  22.2 us (4%)
  between operations  16.1 us (3%)
    psum x1, waiting for transfers between devices, local(): gate_total, up_total = lax.psum((gate_part, up_part), 'shard')  115 us
    reduce_scatter x1, waiting for transfers between devices, local(): lax.psum_scatter(lax.dot_general(columns, latent_codes, (((0,), (1,)), ((...  82 us
    psum x1, blocking collectives, local(): total_square = lax.psum(jnp.sum(errors * errors), ('shard', 'tok'))  71.1 us
    reduce_scatter x1, waiting for transfers between devices, local(): lax.psum_scatter(grad_piece, 'tok', scatter_dimension=1, tiled=True)  69.9 us
    all_gather x2, waiting for transfers between devices, carried_in(): pieces = lax.all_gather(value, axis)  67.1 us
    all_gather x1, waiting for transfers between devices, local(): mlp_full = lax.all_gather(mlp_slice, 'shard', axis=1, tiled=True)  47.5 us
    all_gather x1, waiting for transfers between devices, local(): piece = lax.all_gather(back, 'shard', axis=0, tiled=True)  47 us
    psum x1, blocking collectives, local(): mlp_slice = lax.psum(down_part, 'seg').astype(jnp.bfloat16)  30.9 us
  transfers between devices with their start and end apart: 8, of which 7 were waited for; matrix products, arithmetic and copies ran while one was open for 2% of the time, Pallas kernels for 0%

commit v1 on v0

--- a/solution.py
+++ b/solution.py
@@ -41,7 +41,9 @@
     hidden = (jax.nn.gelu(gate_total, approximate=True) * up_total).astype(jnp.bfloat16)
     down_part = jnp.dot(hidden, down_weight, preferred_element_type=jnp.float32)
     mlp_slice = lax.psum(down_part, "seg").astype(jnp.bfloat16)
-    mlp_full = lax.all_gather(mlp_slice, "shard", axis=1, tiled=True)
+    mlp_full = jnp.concatenate(
+        lax.all_to_all(jnp.stack([mlp_slice] * lax.axis_size("shard")), "shard", 0, 0), axis=1
+    )
     width = mlp_full.shape[1]
     groups = lax.axis_size("tok")
     tokens_all = tok_rows * groups

time: 603 us -> 591 us (0.980)
  waiting for transfers between devices: 428 us -> 405 us
  local copies, waits for them, and re-layouts: 5.01 us -> 12.3 us
    reduce_scatter x1, waiting for transfers between devices: 69.9 us -> 0.02 us  [local(): lax.psum_scatter(grad_piece, 'tok', scatter_dimension=1, tiled=True)]
    reduce_scatter x1, waiting for transfers between devices: 0.02 us -> 69.1 us  [local(): lax.psum_scatter(encoder_grad, 'tok', scatter_dimension=0, tiled=True)]
    all_gather x1 -> x0, waiting for transfers between devices: 47.5 us -> none  [local(): mlp_full = lax.all_gather(mlp_slice, 'shard', axis=1, tiled=True)]
    all_to_all x0 -> x1, waiting for transfers between devices: none -> 20.8 us  [local(): lax.all_to_all(jnp.stack([mlp_slice] * lax.axis_size('shard')), 'shard',...]
where the time goes in v1:
time: 591 us; the launch traced here: 590 us
  waiting for transfers between devices  405 us (69%)
  blocking collectives  101 us (17%)
  matrix products  25.4 us (4%)
  other arithmetic  24.5 us (4%)
  between operations  16.1 us (3%)
  local copies, waits for them, and re-layouts  12.3 us (2%)
    psum x1, waiting for transfers between devices, local(): gate_total, up_total = lax.psum((gate_part, up_part), 'shard')  115 us
    reduce_scatter x1, waiting for transfers between devices, local(): lax.psum_scatter(lax.dot_general(columns, latent_codes, (((0,), (1,)), ((...  86.4 us
    psum x1, blocking collectives, local(): total_square = lax.psum(jnp.sum(errors * errors), ('shard', 'tok'))  70.6 us
    reduce_scatter x1, waiting for transfers between devices, local(): lax.psum_scatter(encoder_grad, 'tok', scatter_dimension=0, tiled=True)  69.1 us
    all_gather x2, waiting for transfers between devices, carried_in(): pieces = lax.all_gather(value, axis)  67.1 us
    all_gather x1, waiting for transfers between devices, local(): piece = lax.all_gather(back, 'shard', axis=0, tiled=True)  47 us
    psum x1, blocking collectives, local(): mlp_slice = lax.psum(down_part, 'seg').astype(jnp.bfloat16)  30.3 us
    all_to_all x1, waiting for transfers between devices, local(): lax.all_to_all(jnp.stack([mlp_slice] * lax.axis_size('shard')), 'shard',...  20.8 us
  transfers between devices with their start and end apart: 8, of which 7 were waited for; matrix products, arithmetic and copies ran while one was open for 2% of the time, Pallas kernels for 0%

profile of v1, /device:TPU:1, one launch (start us, length us, event | category | flops | bytes accessed | tf_op | source)
XLA Modules:
  0.0 590.3 jit_solution(4445514155783429900)
XLA Ops:
  7.2 2.9 fusion.35
  10.2 1.7 fusion.36
  12.0 114.8 %all-reduce.4.cloned.1.call-done = (f32[384,1280]{1,0:T(8,128)}, f32[384,1280]{1,0:T(8,128)}) async-done(((f32[384,1280]{1,0:T(8,128)}, f32[384,1280]{1,0:T(8,128)}), (f32[384,1280]{1,0:T(8,128)}, f32[384,1280]{1,0:T(8,128)})) %all-reduce.4.cloned.1.call-update) | async-done | bytes 3932176 | tf_op jit(solution)/shard_map/psum | solution.py:40
  126.8 3.0 fusion.12
  129.8 30.3 %all-reduce.5 = bf16[384,160]{0,1:T(8,128)(2,1)S(1)} all-reduce(f32[384,160]{0,1:T(8,128)S(1)} %fusion.12), channel_id=1, replica_groups=mesh['seg'=8,'shard'=16,'tok'=2] {'seg'}, use_global_device_ids=true, to_apply=%region_2.0 | all-reduce | flops 61440 | bytes 368640 | tf_op jit(solution)/shard_map/psum | solution.py:43
  160.1 1.4 stack.2
  161.6 5.3 all-to-all-start
  166.9 0.6 fusion.25
  167.6 0.7 add_compare_fusion
  168.2 20.8 %all-to-all-done = bf16[16,384,160]{1,2,0:T(8,128)(2,1)} async-done(((bf16[16,384,160]{1,2,0:T(8,128)(2,1)}), bf16[16,384,160]{1,2,0:T(8,128)(2,1)}, u32[]{:S(2)}, u32[]{:S(2)}) %all-to-all-start) | async-done | bytes 1966112 | tf_op jit(solution)/shard_map/all_to_all | solution.py:45
  189.1 2.1 subtract_convert_fusion
  191.2 0.2 copy-done.9
  191.4 1.2 fusion.9
  192.6 0.1 copy-done.4
  192.7 0.9 copy-done.1
  193.6 3.3 convolution_bitcast_fusion
  197.0 5.5 copy.24
  202.6 86.4 %reduce-scatter.10.cloned.1.call-done = f32[160,384]{1,0:T(8,128)} async-done(((f32[2560,384]{1,0:T(8,128)}), f32[160,384]{1,0:T(8,128)}) %reduce-scatter.10.cloned.1.call-update) | async-done | bytes 245776 | tf_op jit(solution)/shard_map/reduce_scatter | solution.py:63
  289.0 0.1 dynamic_slice.20
  289.1 3.8 convert_element_type.37
  292.9 33.6 %all-gather.8.cloned.1.call-done = f32[1280,384]{1,0:T(8,128)} async-done(((f32[160,384]{1,0:T(8,128)}), f32[1280,384]{1,0:T(8,128)}) %all-gather.8.cloned.1.call-update) | async-done | bytes 1966096 | tf_op jit(solution)/shard_map/all_gather | solution.py:10
  326.5 7.2 %while.28 = (s32[]{:T(128)}, f32[160,384]{1,0:T(8,128)S(1)}, s32[]{:T(128)}, f32[8,160,384]{2,1,0:T(8,128)}, s32[]{:T(128)}, /*index=5*/s32[]{:T(128)}) while((s32[]{:T(128)}, f32[160,384]{1,0:T(8,128)S(1)}, s32[]{:T(128)}, f32[8,160,384]{2,1,0:T(8,128)}, s32[]{:T(128)}, /*index=5*/s32[]{:T(128)}) %tuple.86), condition=%wide.region_6.7_spmd.clone, body=%wide.region_5.6_spmd.clone.sunk | while | flops 184324 | bytes 737373 | solution.py:20
  326.5 1.0 add_select_fusion.4
  327.6 1.0 add_select_fusion.4
  328.6 1.0 add_select_fusion.4
  329.6 1.0 add_select_fusion.4
  330.7 1.0 add_select_fusion.4
  331.7 1.0 add_select_fusion.4
  332.8 1.0 add_select_fusion.4
  333.8 2.3 multiply_reduce_fusion
  336.2 33.5 %all-gather.10.cloned.1.call-done = f32[1280,384]{1,0:T(8,128)} async-done(((f32[160,384]{1,0:T(8,128)}), f32[1280,384]{1,0:T(8,128)}) %all-gather.10.cloned.1.call-update) | async-done | bytes 1966096 | tf_op jit(solution)/shard_map/all_gather | solution.py:10
  369.7 3.0 rev.3
  372.6 7.3 %while.29 = (s32[]{:T(128)}, f32[160,384]{1,0:T(8,128)S(1)}, s32[]{:T(128)}, f32[8,160,384]{2,1,0:T(8,128)}, s32[]{:T(128)}, /*index=5*/s32[]{:T(128)}) while((s32[]{:T(128)}, f32[160,384]{1,0:T(8,128)S(1)}, s32[]{:T(128)}, f32[8,160,384]{2,1,0:T(8,128)}, s32[]{:T(128)}, /*index=5*/s32[]{:T(128)}) %tuple.68), condition=%wide.region_8.9_spmd.clone, body=%wide.region_7.8_spmd.clone.sunk | while | flops 184324 | bytes 737373 | solution.py:20
  372.6 1.1 add_select_fusion.5
  373.7 1.0 add_select_fusion.5
  374.8 1.0 add_select_fusion.5
  375.8 1.0 add_select_fusion.5
  376.8 1.0 add_select_fusion.5
  377.9 1.0 add_select_fusion.5
  378.9 1.0 add_select_fusion.5
  379.9 0.7 multiply_convert_fusion
  380.7 0.0 reduce-scatter.8.cloned.1.call-start
  380.7 47.0 %all-gather.6.cloned.1.call-done = bf16[2560,384]{1,0:T(8,128)(2,1)} async-done(((bf16[160,384]{1,0:T(8,128)(2,1)}), bf16[2560,384]{1,0:T(8,128)(2,1)}) %all-gather.6.cloned.1.call-update) | async-done | bytes 1966096 | tf_op jit(solution)/shard_map/all_gather | solution.py:81
  427.7 5.9 %fusion.32 = f32[512,2560]{1,0:T(8,128)} fusion(bf16[2560,384]{1,0:T(8,128)(2,1)} %all-gather.6.cloned.1.call-done, f32[384,512]{1,0:T(8,128)} %copy-done.1, pred[512]{0:T(512)(128)(4,1)S(1)} %add_compare_fusion), kind=kOutput, calls=%fused_computation.44 | convolution fusion | flops 1008402432 | bytes 7995904 | tf_op jit(solution)/shard_map/dot_general | solution.py:86
  433.7 1.1 copy-done.2
  434.7 7.2 %fusion.11 = f32[2560,512]{1,0:T(8,128)} fusion(bf16[384,2560]{0,1:T(8,128)(2,1)} %copy-done.4, bf16[2560,384]{1,0:T(8,128)(2,1)} %all-gather.6.cloned.1.call-done, bf16[512,2560]{1,0:T(8,128)(2,1)S(1)} %copy-done, f32[384,512]{1,0:T(8,128)S(1)} %copy-done.2, pred[512]{0:T(512)(128)(4,1)S(1)} %add_compare_fusion), kind=kOutput, calls=%fused_computation.19 | convolution fusion | flops 2014445568 | bytes 12583424 | tf_op jit(solution)/shard_map/dot_general | solution.py:90
  442.0 70.6 %psum.31 = f32[]{:T(128)} all-reduce(f32[]{:T(128)} %get-tuple-element.215), channel_id=1, replica_groups=mesh['seg'=8,'shard'=16,'tok'=2] {'shard','tok'}, use_global_device_ids=true, to_apply=%region_12.13 | all-reduce | flops 1 | bytes 8 | tf_op jit(solution)/shard_map/psum | solution.py:77
  513.2 69.1 %reduce-scatter.6.cloned.1.call-done = f32[1280,512]{1,0:T(8,128)} async-done(((f32[2560,512]{1,0:T(8,128)}), f32[1280,512]{1,0:T(8,128)}) %reduce-scatter.6.cloned.1.call-update) | async-done | bytes 2621456 | tf_op jit(solution)/shard_map/reduce_scatter | solution.py:93
  (38 shorter events, 0.4 us)
Async XLA Ops:
  7.2 186.5 %copy-start = (bf16[512,2560]{1,0:T(8,128)(2,1)S(1)}, bf16[512,2560]{1,0:T(8,128)(2,1)}, u32[]{:S(2)}) copy-start(bf16[512,2560]{1,0:T(8,128)(2,1)} %param.19) | copy-start | bytes 7864324
  7.2 3.0 copy-start.6
  7.2 3.0 copy-start.7
  7.2 119.6 %all-reduce.4.cloned.1.call-start = ((), (), s32[]{:S(2)}) async-start(), calls=%async_computation.10 | async-start | bytes 7864320 | tf_op jit(solution)/shard_map/psum | solution.py:40
  11.9 114.8 %copy-start.10 = (bf16[1280,160]{0,1:T(8,128)(2,1)S(1)}, bf16[1280,160]{0,1:T(8,128)(2,1)}, u32[]{:S(2)}) copy-start(bf16[1280,160]{0,1:T(8,128)(2,1)} %param.16) | copy-start | bytes 1228804
  161.6 5.3 copy-start.12
  161.6 27.5 %copy-start.8 = (f32[2560]{0:T(1024)S(1)}, f32[2560]{0:T(1024)}, u32[]{:S(2)}) copy-start(f32[2560]{0:T(1024)} %param.20) | copy-start | bytes 30724
  161.6 27.5 %all-to-all-start = ((bf16[16,384,160]{1,2,0:T(8,128)(2,1)}), bf16[16,384,160]{1,2,0:T(8,128)(2,1)}, u32[]{:S(2)}, u32[]{:S(2)}) async-start(bf16[16,384,160]{1,2,0:T(8,128)(2,1)} %stack.2), calls=%async_computation | async-start | bytes 3932160 | tf_op jit(solution)/shard_map/all_to_all | solution.py:45
  166.9 122.1 %reduce-scatter.10.cloned.1.call-start = ((), (), s32[]{:S(2)}) async-start(), calls=%async_computation.9 | async-start | bytes 4177920 | tf_op jit(solution)/shard_map/reduce_scatter | solution.py:63
  168.2 23.0 %copy-start.11 = (f32[512]{0:T(512)S(1)}, f32[512]{0:T(512)}, u32[]{:S(2)}) copy-start(f32[512]{0:T(512)} %param.18) | copy-start | bytes 6148
  189.1 2.3 copy-start.9
  191.4 1.3 copy-start.4
  192.7 0.9 copy-start.1
  202.5 124.0 %all-gather.8.cloned.1.call-start = ((), (), s32[]{:S(2)}) async-start(), calls=%async_computation.7 | async-start | bytes 2211840 | tf_op jit(solution)/shard_map/all_gather | solution.py:10
  289.0 80.7 %all-gather.10.cloned.1.call-start = ((), (), s32[]{:S(2)}) async-start(), calls=%async_computation.8 | async-start | bytes 2211840 | tf_op jit(solution)/shard_map/all_gather | solution.py:10
  292.9 40.9 %copy-start.5 = (f32[160,384]{1,0:T(8,128)S(1)}, f32[160,384]{1,0:T(8,128)}, u32[]{:S(2)}) copy-start(f32[160,384]{1,0:T(8,128)} %reduce-scatter.10.cloned.1.call-done) | copy-start | bytes 737284
  336.2 91.5 %all-gather.6.cloned.1.call-start = ((), (), s32[]{:S(2)}) async-start(), calls=%async_computation.4 | async-start | bytes 2088960 | tf_op jit(solution)/shard_map/all_gather | solution.py:81
  372.6 7.3 %copy-start.3 = (f32[160,384]{1,0:T(8,128)S(1)}, f32[160,384]{1,0:T(8,128)}, u32[]{:S(2)}) copy-start(f32[160,384]{1,0:T(8,128)} %get-tuple-element.216) | copy-start | bytes 737284
  380.7 132.5 %reduce-scatter.8.cloned.1.call-start = ((), (), s32[]{:S(2)}) async-start(), calls=%async_computation.6 | async-start | bytes 7864320 | tf_op jit(solution)/shard_map/reduce_scatter | solution.py:94
  433.6 1.1 copy-start.2
  433.6 148.7 %reduce-scatter.6.cloned.1.call-start = ((), (), s32[]{:S(2)}) async-start(), calls=%async_computation.5 | async-start | bytes 7864320 | tf_op jit(solution)/shard_map/reduce_scatter | solution.py:93
Sparse Core Ops, SparseCore 0:
  12.1 114.6 all-reduce.3
  202.6 86.2 reduce-scatter.9
  290.8 35.7 all-gather.7
  336.3 33.3 all-gather.9
  380.8 46.8 all-gather.5
  433.8 73.9 reduce-scatter.7
  510.9 71.4 reduce-scatter.5
